TPU v7x, 512 devices: a whole 4x4x16 slice. The times are simulated.
512 devices in a mesh: seq: 64 (over z, x), head: 8 (over y, core).
Axes of the slice: x: 4, y: 4, z: 16, core: 2. Of those that a mesh axis runs over, the one named last changes fastest.
Arguments:
- tokens: bfloat16 [65536, 1024], P('seq'), may hold values from -60 to 60
- qkv_weight: bfloat16 [1024, 8, 384], P(None, 'head'), may hold values from -0.1875 to 0.1875
- out_weight: bfloat16 [8, 128, 1024], P('head'), may hold values from -0.1875 to 0.1875
- members: int32 [8, 256, 768], P('head', None, 'seq'), may hold values from 0 to 65535, as said below
- counts: int32 [8, 64, 256], P('head', 'seq'), may hold values from 1 to 12, as said below
Outputs:
- mixed: bfloat16 [65536, 1024], P(('seq', 'head'))
- centroids: float32 [8, 256, 128], P('head', 'seq')
Inputs may be any that keep to these rules, and one draw needn't show every extreme that they name: `members`: the entries of slots j of any cluster lie in slab j // 12, i.e. in positions 1024 * (j // 12) up to 1024 * (j // 12 + 1) - 1. For each head and slab, the valid entries (j % 12 < counts) over all clusters name every token of that slab exactly once; the other entries are padding with some position of the same slab. For each head and slab the counts over the 256 clusters sum to 1024. For each head, one cluster has 12 members from every slab. Split the 256 clusters into 64 aligned groups of equal size; for each head and slab the counts of one group sum to at most 32, and exactly 32 for the group that holds the full cluster.
All inputs are finite; a program needn't handle non-finite values.
Results may differ from a plain program's by a relative error of at most 0.02.
The roundings to bfloat16 on the way count: a program that leaves them out, or rounds other values in their place, can miss the bound.
Values may be sent and summed in bfloat16 or wider, within the bound.
A program may use at most 128 MiB of HBM per device.

v0:
```python
import jax
import jax.numpy as jnp
from jax import lax
from jax.sharding import PartitionSpec as P

eps_norm = 1e-06


def unit_rows(keys_in):
    widened = keys_in.astype(jnp.float32)
    return widened * lax.rsqrt(jnp.sum(widened * widened, axis=-1, keepdims=True) + eps_norm)


def normalize_rows(sums):
    return sums * lax.rsqrt(jnp.mean(sums * sums, axis=-1, keepdims=True) + eps_norm)


def attend_core(got_rows, got_positions, head_dim, scale):
    seq_count = got_positions.shape[1]
    slab_slots = got_positions.shape[3]
    same_slot = jnp.eye(seq_count * slab_slots, dtype=bool).reshape(
        seq_count, slab_slots, seq_count, slab_slots
    )
    queries = got_rows[..., :head_dim]
    keys_in = got_rows[..., head_dim : 2 * head_dim]
    values_in = got_rows[..., 2 * head_dim :]
    scores = (
        jnp.einsum("hscie,htcje->hcsitj", queries, keys_in, preferred_element_type=jnp.float32)
        * scale
    )
    ordered = jnp.transpose(got_positions, (0, 2, 1, 3))
    query_pos = ordered[:, :, :, :, None, None]
    key_pos = ordered[:, :, None, None, :, :]
    allowed = (key_pos >= 0) & (key_pos <= query_pos) | same_slot[None, None]
    masked = jnp.where(allowed, scores, -1e30)
    highest = jnp.max(masked, axis=(4, 5), keepdims=True)
    expo = jnp.exp(masked - highest)
    probs = (expo / jnp.sum(expo, axis=(4, 5), keepdims=True)).astype(jnp.bfloat16)
    return jnp.einsum(
        "hcsitj,htcje->hscie", probs, values_in, preferred_element_type=jnp.float32
    ).astype(jnp.bfloat16)


def on_device(tokens, qkv_weight, out_weight, members, counts):
    slab_len = tokens.shape[0]
    heads_here = qkv_weight.shape[1]
    head_dim = out_weight.shape[1]
    clusters = members.shape[1]
    slab_slots = members.shape[2]
    seq_count = lax.axis_size("seq")
    owned = clusters // seq_count
    my_slab = lax.axis_index("seq")
    scale = head_dim ** (-0.5)
    projected = jnp.einsum(
        "td,dhe->hte", tokens, qkv_weight, preferred_element_type=jnp.float32
    ).astype(jnp.bfloat16)
    local_ids = members - my_slab * slab_len
    valid = jnp.arange(slab_slots, dtype=jnp.int32)[None, None, :] < counts[:, 0, :, None]
    positions = jnp.where(valid, members, -1)
    member_rows = jax.vmap(lambda table, index: table[index])(projected, local_ids)
    slab_sums = jnp.sum(
        jnp.where(valid[..., None], unit_rows(member_rows[..., head_dim : 2 * head_dim]), 0.0),
        axis=2,
    )
    all_sums = lax.psum(slab_sums, "seq")
    mine = lax.dynamic_slice_in_dim(all_sums, my_slab * owned, owned, 1)
    head_index = jnp.arange(heads_here, dtype=jnp.int32)[:, None, None]
    send_rows = member_rows.reshape(heads_here, seq_count, owned, slab_slots, 3 * head_dim)
    send_positions = positions.reshape(heads_here, seq_count, owned, slab_slots)
    got_rows = lax.all_to_all(send_rows, "seq", split_axis=1, concat_axis=1, tiled=True)
    got_positions = lax.all_to_all(send_positions, "seq", split_axis=1, concat_axis=1, tiled=True)
    attended = attend_core(got_rows, got_positions, head_dim, scale)
    answered = lax.all_to_all(attended, "seq", split_axis=1, concat_axis=1, tiled=True)
    result = answered
    answered = result
    answered = answered.reshape(heads_here, clusters, slab_slots, head_dim)
    target = jnp.where(valid, local_ids, slab_len)
    head_out = (
        jnp.zeros((slab_len, heads_here, head_dim), jnp.bfloat16)
        .at[target, head_index]
        .set(answered, mode="drop")
    )
    centroids = normalize_rows(mine)
    all_heads = lax.all_to_all(head_out, "head", split_axis=0, concat_axis=1, tiled=True)
    mixed = jnp.einsum(
        "the,heo->to",
        all_heads,
        lax.all_gather(out_weight, "head", axis=0, tiled=True),
        preferred_element_type=jnp.float32,
    )
    return (mixed.astype(jnp.bfloat16), centroids)


def solution(mesh):
    return jax.shard_map(
        on_device,
        mesh=mesh,
        in_specs=(
            P("seq", None),
            P(None, "head", None),
            P("head", None, None),
            P("head", None, "seq"),
            P("head", "seq", None),
        ),
        out_specs=(P(("seq", "head"), None), P("head", "seq", None)),
        check_vma=False,
    )
```

profile of v0, /device:TPU:1, one launch (start us, length us, event | category | flops | bytes accessed | tf_op | source)
XLA Modules:
  0.0 421.6 jit_solution(6526205904434901323)
XLA Ops:
  8.0 0.9 compare_select_fusion.2
  8.9 0.8 copy.53
  9.7 19.1 %all-to-all-start.1 = ((s32[1,64,4,12]{3,2,0,1:T(4,128)}), s32[1,64,4,12]{3,2,0,1:T(4,128)S(1)}, u32[]{:S(2)}, u32[]{:S(2)}) async-start(s32[1,64,4,12]{3,2,0,1:T(4,128)} %bitcast.10), calls=%async_computation.1 | async-start | bytes 262144 | tf_op jit(solution)/shard_map/all_to_all | solution.py:71
  28.8 3.0 fusion.5
  31.9 0.1 copy.49
  32.0 0.1 reshape.198
  32.2 1.5 copy.50
  33.7 29.1 %gather_fusion = bf16[3072,384]{1,0:T(8,128)(2,1)} fusion(bf16[1,1024,384]{2,1,0:T(8,128)(2,1)S(1)} %copy.50, s32[3072]{0:T(1024)S(1)} %reshape.198), kind=kCustom, calls=%fused_computation | custom fusion | bytes 4743168 | tf_op jit(solution)/shard_map/vmap()/gather | solution.py:60
  62.8 5.0 %reshape.180 = bf16[1,64,4,12,384]{4,3,2,1,0:T(8,128)(2,1)} reshape(bf16[3072,384]{1,0:T(8,128)(2,1)} %gather_fusion) | data formatting | bytes 4718592 | tf_op jit(solution)/shard_map/reshape | solution.py:68
  67.8 4.2 copy.51
  72.0 14.8 %all-to-all-start = ((bf16[1,64,4,12,384]{4,2,3,0,1:T(4,128)(2,1)}), bf16[1,64,4,12,384]{4,2,3,0,1:T(4,128)(2,1)}, u32[]{:S(2)}, u32[]{:S(2)}) async-start(bf16[1,64,4,12,384]{4,2,3,0,1:T(4,128)(2,1)} %copy.51), calls=%async_computation | async-start | bytes 4718592 | tf_op jit(solution)/shard_map/all_to_all | solution.py:70
  86.7 0.0 all-reduce.3.cloned.1.call-start
  86.8 5.0 %reshape.197 = bf16[1,256,12,384]{3,2,1,0:T(8,128)(2,1)} reshape(bf16[3072,384]{1,0:T(8,128)(2,1)} %gather_fusion) | data formatting | bytes 4718592 | tf_op jit(solution)/shard_map/vmap()/gather | solution.py:60
  91.8 1.8 fusion.2
  93.6 0.1 iota_compare_fusion
  93.8 3.7 fusion.4
  97.5 0.0 all-reduce.3.cloned.1.call-update
  97.5 0.2 all-gather.2.cloned.1.call-start
  97.8 0.3 all-gather.2.cloned.1.call-update
  98.1 1.8 broadcast_compare_fusion
  100.0 0.1 copy.56
  100.1 0.1 broadcast_compare_fusion.1
  100.1 0.1 copy.55
  100.2 93.1 %all-to-all-done = bf16[1,64,4,12,384]{4,2,3,0,1:T(4,128)(2,1)} async-done(((bf16[1,64,4,12,384]{4,2,3,0,1:T(4,128)(2,1)}), bf16[1,64,4,12,384]{4,2,3,0,1:T(4,128)(2,1)}, u32[]{:S(2)}, u32[]{:S(2)}) %all-to-all-start) | async-done | bytes 2359328 | tf_op jit(solution)/shard_map/all_to_all | solution.py:70
  193.3 3.3 fusion.16
  196.6 10.4 %fusion.17 = (f32[4,64,12]{1,2,0:T(8,128)S(1)}, f32[4,64,12,64,12]{1,3,4,2,0:T(8,128)}) fusion(bf16[1,64,4,12,128]{4,2,3,0,1:T(4,128)(2,1)S(1)} %get-tuple-element.4, bf16[1,64,4,12,128]{4,2,3,0,1:T(4,128)(2,1)S(1)} %get-tuple-element.3, pred[64,12,64,12]{0,2,3,1:T(8,128)(4,1)S(1)} %copy-done.1, s32[4,64,12]{1,2,0:T(8,128)S(1)} %copy.56, ...), kind=kOutput, calls=%fused_computation.48 | convolution fusion | flops 618132480 | bytes 11627520 | tf_op jit(solution)/shard_map/hscie,htcje->hcsitj/dot_general | solution.py:28
  207.0 10.2 %fusion = f32[4,64,12]{1,2,0:T(8,128)S(1)} fusion(f32[4,64,12,64,12]{1,3,4,2,0:T(8,128)} %get-tuple-element.9, f32[4,64,12]{1,2,0:T(8,128)S(1)} %get-tuple-element.8), kind=kLoop, calls=%fused_computation.5 | loop fusion | flops 4715520 | bytes 9461760 | tf_op jit(solution)/shard_map/reduce_sum | solution.py:38
  217.2 8.5 %fusion.6 = bf16[1,64,4,12,128]{4,1,3,2,0:T(8,128)(2,1)S(1)} fusion(f32[4,64,12,64,12]{1,3,4,2,0:T(8,128)} %get-tuple-element.9, f32[4,64,12]{1,2,0:T(8,128)S(1)} %fusion, f32[4,64,12]{1,2,0:T(8,128)S(1)} %get-tuple-element.8, bf16[1,64,4,12,128]{4,2,3,0,1:T(4,128)(2,1)S(1)} %copy-done.2), kind=kOutput, calls=%fused_computation.16 | convolution fusion | flops 611450880 | bytes 11034624 | tf_op jit(solution)/shard_map/hcsitj,htcje->hscie/dot_general | solution.py:39
  225.8 1.5 copy.61
  227.3 11.4 %all-to-all-start.2 = ((bf16[1,64,4,12,128]{4,2,3,0,1:T(4,128)(2,1)}), bf16[1,64,4,12,128]{4,2,3,0,1:T(4,128)(2,1)}, u32[]{:S(2)}, u32[]{:S(2)}) async-start(bf16[1,64,4,12,128]{4,2,3,0,1:T(4,128)(2,1)} %copy.61), calls=%async_computation.2 | async-start | bytes 1572864 | tf_op jit(solution)/shard_map/all_to_all | solution.py:73
  238.7 0.1 multiply_reduce_fusion
  238.8 0.1 and_reduce_fusion
  238.9 0.1 copy.48
  239.0 0.1 reshape.206
  239.2 136.0 %all-reduce.3.cloned.1.call-done = f32[1,256,128]{2,1,0:T(8,128)} async-done(((f32[1,256,128]{2,1,0:T(8,128)}), f32[1,256,128]{2,1,0:T(8,128)}) %all-reduce.3.cloned.1.call-update) | async-done | bytes 131088 | tf_op jit(solution)/shard_map/psum | solution.py:65
  375.2 0.8 multiply_reduce_fusion.1
  376.0 1.4 copy.62
  377.4 1.1 reshape.208
  378.4 8.6 %scatter_custom_fusion = bf16[1024,128]{1,0:T(8,128)(2,1)S(1)} fusion(s32[3072]{0:T(1024)S(1)} %reshape.206, bf16[3072,128]{1,0:T(8,128)(2,1)} %reshape.208, bf16[]{:T(256)} %constant.15.clone.1), kind=kCustom, calls=%fused_computation.23 | custom fusion | bytes 262656
  387.1 0.5 broadcast.148
  387.6 0.8 reduce.13
  388.4 0.8 reshape.225
  389.2 15.4 %all-to-all-start.3 = ((bf16[8,2,8192]{2,1,0:T(2,128)(2,1)}), bf16[8,2,8192]{2,1,0:T(2,128)(2,1)S(1)}, u32[]{:S(2)}, u32[]{:S(2)}) async-start(bf16[8,2,8192]{2,1,0:T(2,128)(2,1)} %reshape.225), calls=%async_computation.3 | async-start | bytes 524288 | tf_op jit(solution)/shard_map/all_to_all | solution.py:84
  404.6 1.3 dynamic-slice_multiply_fusion
  405.9 5.2 %all-to-all-done.3 = bf16[8,2,8192]{2,1,0:T(2,128)(2,1)S(1)} async-done(((bf16[8,2,8192]{2,1,0:T(2,128)(2,1)}), bf16[8,2,8192]{2,1,0:T(2,128)(2,1)S(1)}, u32[]{:S(2)}, u32[]{:S(2)}) %all-to-all-start.3) | async-done | bytes 262176 | tf_op jit(solution)/shard_map/all_to_all | solution.py:84
  411.1 0.3 reshape.226
  411.4 0.0 all-gather.2.cloned.1.call-done
  411.4 2.7 fusion.7
  (21 shorter events, 0.2 us)
Async XLA Ops:
  8.0 20.8 %copy-start = (bf16[1024,1024]{1,0:T(8,128)(2,1)S(1)}, bf16[1024,1024]{1,0:T(8,128)(2,1)}, u32[]{:S(2)}) copy-start(bf16[1024,1024]{1,0:T(8,128)(2,1)} %param.5) | copy-start | bytes 6291460
  9.7 62.3 %all-to-all-start.1 = ((s32[1,64,4,12]{3,2,0,1:T(4,128)}), s32[1,64,4,12]{3,2,0,1:T(4,128)S(1)}, u32[]{:S(2)}, u32[]{:S(2)}) async-start(s32[1,64,4,12]{3,2,0,1:T(4,128)} %bitcast.10), calls=%async_computation.1 | async-start | bytes 262144 | tf_op jit(solution)/shard_map/all_to_all | solution.py:71
  72.0 121.4 %all-to-all-start = ((bf16[1,64,4,12,384]{4,2,3,0,1:T(4,128)(2,1)}), bf16[1,64,4,12,384]{4,2,3,0,1:T(4,128)(2,1)}, u32[]{:S(2)}, u32[]{:S(2)}) async-start(bf16[1,64,4,12,384]{4,2,3,0,1:T(4,128)(2,1)} %copy.51), calls=%async_computation | async-start | bytes 4718592 | tf_op jit(solution)/shard_map/all_to_all | solution.py:70
  86.7 6.9 %copy-start.3 = (s32[1,1,256]{2,1,0:T(1,128)S(1)}, s32[1,1,256]{2,1,0:T(1,128)}, u32[]{:S(2)}) copy-start(s32[1,1,256]{2,1,0:T(1,128)} %param.9) | copy-start | bytes 3076
  86.7 288.4 %all-reduce.3.cloned.1.call-start = ((), (), s32[]{:S(2)}) async-start(), calls=%async_computation.5 | async-start | bytes 262144 | tf_op jit(solution)/shard_map/psum | solution.py:65
  97.5 313.9 %all-gather.2.cloned.1.call-start = ((), (), s32[]{:S(2)}) async-start(), calls=%async_computation.4 | async-start | bytes 2359296 | tf_op jit(solution)/shard_map/all_gather | solution.py:88
  100.2 96.4 %copy-start.1 = (pred[64,12,64,12]{0,2,3,1:T(8,128)(4,1)S(1)}, pred[64,12,64,12]{0,2,3,1:T(8,128)(4,1)}, u32[]{:S(2)}) copy-start(pred[64,12,64,12]{0,2,3,1:T(8,128)(4,1)} %broadcast_compare_fusion) | copy-start | bytes 1769476
  207.0 10.2 %copy-start.2 = (bf16[1,64,4,12,128]{4,2,3,0,1:T(4,128)(2,1)S(1)}, bf16[1,64,4,12,128]{4,2,3,0,1:T(4,128)(2,1)}, u32[]{:S(2)}) copy-start(bf16[1,64,4,12,128]{4,2,3,0,1:T(4,128)(2,1)} %get-tuple-element.2) | copy-start | bytes 2359300
  225.7 12.9 %copy-start.4 = (s32[2]{0:T(128)S(1)}, s32[2]{0:T(128)}, u32[]{:S(2)}) copy-start(s32[2]{0:T(128)} %constant.45) | copy-start | bytes 28
  225.7 13.0 %copy-start.5 = (s32[2]{0:T(128)S(1)}, s32[2]{0:T(128)}, u32[]{:S(2)}) copy-start(s32[2]{0:T(128)} %constant.48) | copy-start | bytes 28
  227.3 148.7 %all-to-all-start.2 = ((bf16[1,64,4,12,128]{4,2,3,0,1:T(4,128)(2,1)}), bf16[1,64,4,12,128]{4,2,3,0,1:T(4,128)(2,1)}, u32[]{:S(2)}, u32[]{:S(2)}) async-start(bf16[1,64,4,12,128]{4,2,3,0,1:T(4,128)(2,1)} %copy.61), calls=%async_computation.2 | async-start | bytes 1572864 | tf_op jit(solution)/shard_map/all_to_all | solution.py:73
  389.2 21.9 %all-to-all-start.3 = ((bf16[8,2,8192]{2,1,0:T(2,128)(2,1)}), bf16[8,2,8192]{2,1,0:T(2,128)(2,1)S(1)}, u32[]{:S(2)}, u32[]{:S(2)}) async-start(bf16[8,2,8192]{2,1,0:T(2,128)(2,1)} %reshape.225), calls=%async_computation.3 | async-start | bytes 524288 | tf_op jit(solution)/shard_map/all_to_all | solution.py:84
Sparse Core Ops, SparseCore 0:
  97.6 277.4 all-reduce.2
Sparse Core Ops, SparseCore 1:
  100.1 35.2 all-gather.1
where the time goes:
time: 423 us; the launch traced here: 422 us
  waiting for transfers between devices  235 us (56%)
  local copies, waits for them, and re-layouts  63.8 us (15%)
  starting transfers between devices  60.9 us (14%)
  matrix products  24.6 us (6%)
  other arithmetic  21.9 us (5%)
  between operations  15.7 us (4%)
    psum x1, waiting for transfers between devices, on_device(): all_sums = lax.psum(slab_sums, 'seq')  136 us
    all_to_all x1, waiting for transfers between devices, on_device(): lax.all_to_all(send_rows, 'seq', split_axis=1, concat_axis=1, tiled=True)  93.1 us
    gather x4, local copies, waits for them, and re-layouts, on_device(): table[index]  34.3 us
    all_to_all x1, starting transfers between devices, on_device(): lax.all_to_all(send_positions, 'seq', split_axis=1, concat_axis=1, tiled=...  19.1 us
    all_to_all x1, starting transfers between devices, on_device(): lax.all_to_all(head_out, 'head', split_axis=0, concat_axis=1, tiled=True)  15.4 us
    all_to_all x1, starting transfers between devices, on_device(): lax.all_to_all(send_rows, 'seq', split_axis=1, concat_axis=1, tiled=True)  14.8 us
    all_to_all x1, starting transfers between devices, on_device(): lax.all_to_all(attended, 'seq', split_axis=1, concat_axis=1, tiled=True)  11.4 us
    dot_general x1, matrix products, attend_core(): jnp.einsum('hscie,htcje->hcsitj', queries, keys_in, preferred_element_typ...  10.4 us
  transfers between devices with their start and end apart: 6, of which 3 were waited for; matrix products, arithmetic and copies ran while one was open for 25% of the time, Pallas kernels for 0%

commit v1 on v0

v1 whole, which is shorter than its diff:
```python
import functools

import jax
import jax.numpy as jnp
from jax import lax
from jax.experimental import pallas as pl
from jax.experimental.pallas import tpu as pltpu
from jax.sharding import PartitionSpec as P

MESH = pl.DeviceIdType.MESH
eps_norm = 1e-06
f32, bf16, i32 = jnp.float32, jnp.bfloat16, jnp.int32


def iota(shape, dim):
    return lax.broadcasted_iota(i32, shape, dim)


def nt_dot(a, b):
    return lax.dot_general(a, b, (((1,), (1,)), ((), ())), preferred_element_type=f32)


def layer_kernel(
    nx, batch, q_rows,
    tokens, wqkv, wo, slot_ids, cnt,
    mixed, cent,
    proj, pick, put, qk_s, v_s, qk_r, v_r, probs, o_s, o_r, acc, hs, hr, wo_r,
    cnt_s, tab_r, tab, held, cl_col,
    send_sem, cnt_sem, qk_sem, v_sem, o_sem, h_sem, wo_sem,
):
    n, heads = lax.axis_size("seq"), lax.axis_size("head")
    me, my_head = lax.axis_index("seq"), lax.axis_index("head")
    nz = n // nx
    my_z, my_x = me // nx, lax.rem(me, nx)
    slab, hd = proj.shape[0], wo.shape[0]
    cap = qk_s.shape[0] // n
    clusters = cnt.shape[1]
    owned = clusters // n
    s_c = slot_ids.shape[0]
    batches = n // batch
    rows_b = batch * cap
    out_rows = mixed.shape[0]

    def peer(step):
        dz = lax.rem((step // nx) * 7, nz)
        return lax.rem(my_z + dz, nz) * nx + lax.rem(my_x + lax.rem(step, nx), nx)

    def block(ref, index, size):
        return ref.at[pl.ds(pl.multiple_of(index * size, size), size), :]

    def remote(src, dst, ssem, rsem, where):
        return pltpu.make_async_remote_copy(
            src_ref=src, dst_ref=dst, send_sem=ssem, recv_sem=rsem,
            device_id=where, device_id_type=MESH,
        )

    barrier = pltpu.get_barrier_semaphore()

    @pl.loop(1, n)
    def _(step):
        pl.semaphore_signal(barrier, inc=1, device_id={"seq": peer(step)}, device_id_type=MESH)

    @pl.loop(1, heads)
    def _(step):
        pl.semaphore_signal(
            barrier, inc=1, device_id={"head": lax.rem(my_head + step, heads)}, device_id_type=MESH
        )

    local = slot_ids[...] - me * slab
    count = cnt[...]
    rank = jnp.zeros((s_c, clusters), i32)
    for j in range(s_c):
        rank += jnp.where((local[j : j + 1, :] < local) & (count > j), 1, 0)
    wide = jnp.broadcast_to(count, (8, clusters))
    lane4 = lax.rem(iota((8, clusters), 1), owned)
    start = jnp.zeros((8, clusters), i32)
    for k in range(1, owned):
        start += jnp.where(lane4 >= k, pltpu.roll(wide, k, 1), 0)
    slot = jnp.where(iota((s_c, clusters), 0) < count, rank + start[:1, :], -1)
    token = jnp.zeros((cap, clusters), f32)
    row = iota((cap, clusters), 0)
    for j in range(s_c):
        token += jnp.where(slot[j : j + 1, :] == row, (local[j : j + 1, :] + 1).astype(f32), 0.0)
    total = token
    for k in range(1, owned):
        total += pltpu.roll(token, clusters - k, 1)
    held[...] = total
    cnt_s[...] = count.astype(f32)

    proj[...] = jnp.dot(tokens[...], wqkv[...], preferred_element_type=f32).astype(bf16)

    pl.semaphore_wait(barrier, n - 1 + heads - 1)

    @pl.loop(1, n)
    def _(step):
        remote(cnt_s, tab_r.at[me], send_sem.at[0], cnt_sem, {"seq": peer(step)}).start()

    pltpu.make_async_copy(cnt_s, tab_r.at[me], cnt_sem).start()

    def send_qk(step):
        remote(block(qk_s, step, cap), block(qk_r, me, cap), send_sem.at[1], qk_sem,
               {"seq": peer(step)}).start()

    def send_v(step):
        remote(block(v_s, step, cap), block(v_r, me, cap), send_sem.at[2], v_sem,
               {"seq": peer(step)}).start()

    col = iota((cap, slab), 1)
    lane = iota((cap, clusters), 1)

    @pl.loop(0, batches)
    def _(b):
        @pl.loop(0, batch)
        def _(i):
            step = b * batch + i
            mine = jnp.sum(
                jnp.where(lane == owned * peer(step), held[...], 0.0), axis=1, keepdims=True
            )
            hit = jnp.where((col + 1).astype(f32) == mine, 1.0, 0.0)
            pick[pl.ds(pl.multiple_of(step * cap, cap), cap), :] = hit.astype(bf16)

        at = pl.ds(pl.multiple_of(b * rows_b, rows_b), rows_b)
        rows = jnp.dot(pick[at, :], proj[...], preferred_element_type=f32).astype(bf16)
        qk_s[at, :] = rows[:, : 2 * hd]
        v_s[at, :] = rows[:, 2 * hd :]

        @pl.loop(0, batch)
        def _(i):
            step = b * batch + i

            @pl.when(step > 0)
            def _():
                send_qk(step)

    pltpu.make_async_copy(block(qk_s, 0, cap), block(qk_r, me, cap), qk_sem).start()

    @pl.loop(1, n)
    def _(step):
        send_v(step)

    pltpu.make_async_copy(block(v_s, 0, cap), block(v_r, me, cap), v_sem).start()

    @pl.loop(1, heads)
    def _(step):
        remote(wo, block(wo_r, my_head, hd), send_sem.at[3], wo_sem,
               {"head": lax.rem(my_head + step, heads)}).start()

    pltpu.make_async_copy(wo, block(wo_r, my_head, hd), wo_sem).start()

    for b in range(batches):
        part = pick[b * rows_b : (b + 1) * rows_b, :].astype(f32)
        put[:, b * rows_b : (b + 1) * rows_b] = part.T.astype(bf16)

    pltpu.make_async_copy(tab_r, tab_r, cnt_sem).wait()

    @pl.loop(0, n)
    def _(s):
        tab[pl.ds(s, 1), :] = tab_r[s]

    table = tab[...].astype(bf16)

    def ends(rows_k):
        k_id, c_id = iota((rows_k, clusters), 0), iota((rows_k, clusters), 1)
        inside = (c_id // owned == me) & (lax.rem(c_id, owned) <= k_id)
        return jnp.where(inside, 1.0, 0.0).astype(bf16)

    total_rows = n * cap
    spread_t = jnp.where(iota((n, total_rows), 1) // cap == iota((n, total_rows), 0), 1.0, 0.0)
    end_row = jnp.dot(
        nt_dot(ends(8), table).astype(bf16), spread_t.astype(bf16), preferred_element_type=f32
    )
    past = (lax.rem(iota((8, total_rows), 1), cap).astype(f32) >= end_row) & (
        iota((8, total_rows), 0) < owned
    )
    cl_row = jnp.sum(jnp.where(past, 1.0, 0.0), axis=0, keepdims=True)
    spread = jnp.where(iota((total_rows, n), 0) // cap == iota((total_rows, n), 1), 1.0, 0.0)
    end_col = jnp.dot(
        spread.astype(bf16), nt_dot(table, ends(128)).astype(bf16), preferred_element_type=f32
    )
    past = (lax.rem(iota((total_rows, 128), 0), cap).astype(f32) >= end_col) & (
        iota((total_rows, 128), 1) < owned
    )
    cl_col[...] = jnp.sum(jnp.where(past, 1.0, 0.0), axis=1, keepdims=True)

    pltpu.make_async_copy(qk_r, qk_r, qk_sem).wait()
    scale = hd ** (-0.5)

    @pl.loop(0, total_rows // q_rows)
    def _(c):
        at = pl.ds(pl.multiple_of(c * q_rows, q_rows), q_rows)
        scores = nt_dot(qk_r[at, :hd], qk_r[:, hd:]) * scale
        ahead = iota((q_rows, total_rows), 1) <= iota((q_rows, total_rows), 0) + c * q_rows
        allowed = (cl_col[at, :] == cl_row) & ahead
        masked = jnp.where(allowed, scores, -1e30)
        expo = jnp.exp(masked - jnp.max(masked, axis=1, keepdims=True))
        probs[at, :] = (expo / jnp.sum(expo, axis=1, keepdims=True)).astype(bf16)

    sums = [jnp.zeros((1, hd), f32) for _ in range(owned)]
    keys = qk_r[:, hd:].astype(f32)
    unit = keys * lax.rsqrt(jnp.sum(keys * keys, axis=1, keepdims=True) + eps_norm)
    for k in range(owned):
        kept = jnp.where(cl_col[...] == float(k), unit, 0.0)
        one = jnp.sum(kept, axis=0, keepdims=True)
        cent[k : k + 1, :] = one * lax.rsqrt(jnp.mean(one * one, axis=1, keepdims=True) + eps_norm)

    pltpu.make_async_copy(v_r, v_r, v_sem).wait()

    @pl.loop(0, batches)
    def _(b):
        turn = lax.rem(my_z * nx // batch + 3 * b, batches)
        at = pl.ds(pl.multiple_of(turn * rows_b, rows_b), rows_b)
        o_s[at, :] = jnp.dot(probs[at, :], v_r[...], preferred_element_type=f32).astype(bf16)

        @pl.loop(0, batch)
        def _(i):
            s = turn * batch + i
            step = (
                lax.rem(7 * lax.rem(my_z - s // nx + nz, nz), nz) * nx
                + lax.rem(my_x - lax.rem(s, nx) + nx, nx)
            )

            @pl.when(s != me)
            def _():
                remote(block(o_s, s, cap), block(o_r, step, cap), send_sem.at[4],
                       o_sem.at[step // batch], {"seq": s}).start()

            @pl.when(s == me)
            def _():
                pltpu.make_async_copy(
                    block(o_s, s, cap), block(o_r, step, cap), o_sem.at[step // batch]
                ).start()

    acc[...] = jnp.zeros_like(acc)
    for b in range(batches):
        at = pl.ds(b * rows_b, rows_b)
        pltpu.make_async_copy(o_r.at[at, :], o_r.at[at, :], o_sem.at[b]).wait()
        acc[...] += jnp.dot(put[:, b * rows_b : (b + 1) * rows_b], o_r[at, :],
                            preferred_element_type=f32)
    hs[...] = acc[...].astype(bf16)

    @pl.loop(1, heads)
    def _(step):
        to = lax.rem(my_head + step, heads)
        remote(block(hs, to, out_rows), hr.at[my_head], send_sem.at[5], h_sem,
               {"head": to}).start()

    pltpu.make_async_copy(block(hs, my_head, out_rows), hr.at[my_head], h_sem).start()
    pltpu.make_async_copy(wo_r, wo_r, wo_sem).wait()
    pltpu.make_async_copy(hr, hr, h_sem).wait()
    all_heads = jnp.concatenate([hr[h] for h in range(heads)], axis=1)
    mixed[...] = jnp.dot(all_heads, wo_r[...], preferred_element_type=f32).astype(bf16)

    def sent(ref, index):
        pltpu.make_async_copy(ref, ref, send_sem.at[index]).wait()

    sent(tab_r.at[pl.ds(0, n - 1)], 0)
    sent(qk_s.at[pl.ds(0, (n - 1) * cap), :], 1)
    sent(v_s.at[pl.ds(0, (n - 1) * cap), :], 2)
    sent(wo_r.at[pl.ds(0, (heads - 1) * hd), :], 3)
    sent(o_s.at[pl.ds(0, (n - 1) * cap), :], 4)
    sent(hr.at[pl.ds(0, heads - 1)], 5)


def on_device(nx, tokens, qkv_weight, out_weight, members, counts):
    slab, width = tokens.shape
    heads, n = lax.axis_size("head"), lax.axis_size("seq")
    hd = out_weight.shape[1]
    clusters, s_c = members.shape[1], members.shape[2]
    cap = 2 * slab // n
    rows = n * cap
    batch = min(8, n // 2)
    vm = lambda shape, dtype: pltpu.VMEM(shape, dtype)
    mixed, centroids = pl.pallas_call(
        functools.partial(layer_kernel, nx, batch, 128),
        out_shape=(
            jax.ShapeDtypeStruct((slab // heads, width), bf16),
            jax.ShapeDtypeStruct((clusters // n, hd), f32),
        ),
        in_specs=[pl.BlockSpec(memory_space=pltpu.VMEM)] * 5,
        out_specs=(pl.BlockSpec(memory_space=pltpu.VMEM),) * 2,
        scratch_shapes=[
            vm((slab, 3 * hd), bf16),
            vm((rows, slab), bf16),
            vm((slab, rows), bf16),
            vm((rows, 2 * hd), bf16),
            vm((rows, hd), bf16),
            vm((rows, 2 * hd), bf16),
            vm((rows, hd), bf16),
            vm((rows, rows), bf16),
            vm((rows, hd), bf16),
            vm((rows, hd), bf16),
            vm((slab, hd), f32),
            vm((slab, hd), bf16),
            vm((heads, slab // heads, hd), bf16),
            vm((heads * hd, width), bf16),
            vm((1, clusters), f32),
            vm((n, 1, clusters), f32),
            vm((n, clusters), f32),
            vm((cap, clusters), f32),
            vm((rows, 1), f32),
            pltpu.SemaphoreType.DMA((6,)),
            pltpu.SemaphoreType.DMA,
            pltpu.SemaphoreType.DMA,
            pltpu.SemaphoreType.DMA,
            pltpu.SemaphoreType.DMA((n // batch,)),
            pltpu.SemaphoreType.DMA,
            pltpu.SemaphoreType.DMA,
        ],
        compiler_params=pltpu.CompilerParams(
            collective_id=0, has_side_effects=True, vmem_limit_bytes=56 << 20
        ),
    )(
        tokens,
        qkv_weight.reshape(width, 3 * hd),
        out_weight.reshape(hd, width),
        members.reshape(clusters, s_c).T,
        counts.reshape(1, clusters),
    )
    return mixed, centroids[None]


def solution(mesh):
    n = mesh.shape["seq"]
    return jax.shard_map(
        functools.partial(on_device, min(4, n // 4)),
        mesh=mesh,
        in_specs=(
            P("seq", None),
            P(None, "head", None),
            P("head", None, None),
            P("head", None, "seq"),
            P("head", "seq", None),
        ),
        out_specs=(P(("seq", "head"), None), P("head", "seq", None)),
        check_vma=False,
    )
```

time: 423 us -> 135 us (0.32)
  waiting for transfers between devices: 235 us -> 0 us
  Pallas kernels: 0 us -> 130 us
  starting transfers between devices: 60.9 us -> 0 us
  local copies, waits for them, and re-layouts: 63.8 us -> 4.23 us
  matrix products: 24.6 us -> 0 us
  other arithmetic: 21.9 us -> 0 us
  between operations: 15.7 us -> 0.64 us
    psum x1 -> x0, waiting for transfers between devices: 136 us -> none  [on_device(): all_sums = lax.psum(slab_sums, 'seq')]
    pallas_call x0 -> x1, Pallas kernels: none -> 130 us  [on_device(): pl.pallas_call(functools.partial(layer_kernel, nx, batch, 128), out_shape...]
    all_to_all x4 -> x0, waiting for transfers between devices: 98.3 us -> none  [the longest x1 93.1 us: on_device(): lax.all_to_all(send_rows, 'seq', split_axis=1, concat_axis=1, tiled=True)]
    all_to_all x4 -> x0, starting transfers between devices: 60.7 us -> none  [the longest x1 19.1 us: on_device(): lax.all_to_all(send_positions, 'seq', split_axis=1, concat_axis=1, tiled=...]
    gather x4 -> x0, local copies, waits for them, and re-layouts: 34.3 us -> none  [on_device(): table[index]]
    dot_general x4 -> x0, matrix products: 24.6 us -> none  [the longest x1 10.4 us: attend_core(): jnp.einsum('hscie,htcje->hcsitj', queries, keys_in, preferred_element_typ...]
    reduce_sum x4 -> x0, other arithmetic: 16.6 us -> none  [the longest x1 10.2 us: attend_core(): jnp.sum(expo, axis=(4, 5), keepdims=True)]
    reshape x3 -> x0, local copies, waits for them, and re-layouts: 10.2 us -> none  [the longest x2 9.17 us: on_device(): member_rows.reshape(heads_here, seq_count, owned, slab_slots, 3 * head_dim)]
  transfers between devices with their start and end apart: 6 -> 0, of which waited for: 3 -> 0; matrix products, arithmetic and copies ran while one was open for 25% -> 0% of each run, Pallas kernels for 0% -> 0%
where the time goes in v1:
time: 135 us
  Pallas kernels  130 us (96%)
  local copies, waits for them, and re-layouts  4.23 us (3%)
    pallas_call x1, Pallas kernels, on_device(): pl.pallas_call(functools.partial(layer_kernel, nx, batch, 128), out_shape...  130 us
    unnamed x3, local copies, waits for them, and re-layouts  4.23 us

profile of v1, /device:TPU:1, one launch (start us, length us, event | category | flops | bytes accessed | tf_op | source)
XLA Modules:
  0.0 134.9 jit_solution(16743966059214166755)
XLA Ops:
  0.6 1.3 copy.9
  1.9 130.0 %shard_map.68 = (bf16[128,1024]{1,0:T(8,128)(2,1)}, f32[4,128]{1,0:T(4,128)}) custom-call(bf16[1024,1024]{1,0:T(8,128)(2,1)} %tokens.1, bf16[1024,384]{1,0:T(8,128)(2,1)} %bitcast.9, bf16[128,1024]{1,0:T(8,128)(2,1)} %bitcast.10, s32[12,256]{1,0:T(8,128)} %bitcast.11, s32[1,256]{1,0:T(1,128)} %bitcast.13), custom_call_target="tpu_custom_call" | custom-call | tf_op jit(solution)/shard_map/pallas_call | solution.py:273
  132.0 1.7 %copy.12 = bf16[128,1024]{1,0:T(8,128)(2,1)} copy(bf16[128,1024]{1,0:T(8,128)(2,1)} %get-tuple-element.8) | data formatting | bytes 524288
  133.7 1.2 copy.13

commit v2 on v1

--- a/solution.py
+++ b/solution.py
@@ -22,11 +22,11 @@
 
 def layer_kernel(
     nx, batch, q_rows,
-    tokens, wqkv, wo, slot_ids, cnt,
-    mixed, cent,
-    proj, pick, put, qk_s, v_s, qk_r, v_r, probs, o_s, o_r, acc, hs, hr, wo_r,
+    tokens_hbm, wqkv_hbm, wo, ids_hbm, cnt_hbm,
+    all_heads, all_wo, cent,
+    tokens, wqkv, ids, cnt, proj, pick, put, qk_s, v_s, qk_r, v_r, probs, o_s, o_r, acc, hs,
     cnt_s, tab_r, tab, held, cl_col,
-    send_sem, cnt_sem, qk_sem, v_sem, o_sem, h_sem, wo_sem,
+    in_sem, send_sem, cnt_sem, qk_sem, v_sem, o_sem, h_sem, wo_sem,
 ):
     n, heads = lax.axis_size("seq"), lax.axis_size("head")
     me, my_head = lax.axis_index("seq"), lax.axis_index("head")
@@ -35,15 +35,23 @@
     slab, hd = proj.shape[0], wo.shape[0]
     cap = qk_s.shape[0] // n
     clusters = cnt.shape[1]
+    pairs = nz // 2
+    my_pair, my_odd = my_z // 2, lax.rem(my_z, 2)
     owned = clusters // n
-    s_c = slot_ids.shape[0]
+    s_c = ids.shape[0]
     batches = n // batch
     rows_b = batch * cap
-    out_rows = mixed.shape[0]
+    out_rows = all_heads.shape[0]
+
+    def offset(b):
+        return pairs // 2 + (b + 1) // 2 * (1 - 2 * lax.rem(b, 2))
+
+    own_step = (batches - 1) * batch
 
     def peer(step):
-        dz = lax.rem((step // nx) * 7, nz)
-        return lax.rem(my_z + dz, nz) * nx + lax.rem(my_x + lax.rem(step, nx), nx)
+        b, i = step // batch, lax.rem(step, batch)
+        pair = lax.rem(my_pair + offset(b), pairs)
+        return (pair * 2 + lax.rem(my_odd + i // nx, 2)) * nx + lax.rem(my_x + i, nx)
 
     def block(ref, index, size):
         return ref.at[pl.ds(pl.multiple_of(index * size, size), size), :]
@@ -54,11 +62,22 @@
             device_id=where, device_id_type=MESH,
         )
 
+    loads = [
+        pltpu.make_async_copy(ids_hbm, ids, in_sem.at[0]),
+        pltpu.make_async_copy(cnt_hbm, cnt, in_sem.at[1]),
+        pltpu.make_async_copy(wqkv_hbm, wqkv, in_sem.at[2]),
+        pltpu.make_async_copy(tokens_hbm, tokens, in_sem.at[3]),
+    ]
+    for load in loads:
+        load.start()
+
     barrier = pltpu.get_barrier_semaphore()
 
     @pl.loop(1, n)
     def _(step):
-        pl.semaphore_signal(barrier, inc=1, device_id={"seq": peer(step)}, device_id_type=MESH)
+        pl.semaphore_signal(
+            barrier, inc=1, device_id={"seq": lax.rem(me + step, n)}, device_id_type=MESH
+        )
 
     @pl.loop(1, heads)
     def _(step):
@@ -66,7 +85,9 @@
             barrier, inc=1, device_id={"head": lax.rem(my_head + step, heads)}, device_id_type=MESH
         )
 
-    local = slot_ids[...] - me * slab
+    loads[0].wait()
+    loads[1].wait()
+    local = jnp.concatenate([ids[j] for j in range(s_c)], axis=0) - me * slab
     count = cnt[...]
     rank = jnp.zeros((s_c, clusters), i32)
     for j in range(s_c):
@@ -87,36 +108,16 @@
     held[...] = total
     cnt_s[...] = count.astype(f32)
 
-    proj[...] = jnp.dot(tokens[...], wqkv[...], preferred_element_type=f32).astype(bf16)
-
-    pl.semaphore_wait(barrier, n - 1 + heads - 1)
-
-    @pl.loop(1, n)
-    def _(step):
-        remote(cnt_s, tab_r.at[me], send_sem.at[0], cnt_sem, {"seq": peer(step)}).start()
-
-    pltpu.make_async_copy(cnt_s, tab_r.at[me], cnt_sem).start()
-
-    def send_qk(step):
-        remote(block(qk_s, step, cap), block(qk_r, me, cap), send_sem.at[1], qk_sem,
-               {"seq": peer(step)}).start()
-
-    def send_v(step):
-        remote(block(v_s, step, cap), block(v_r, me, cap), send_sem.at[2], v_sem,
-               {"seq": peer(step)}).start()
-
-    col = iota((cap, slab), 1)
+    col = (iota((cap, slab), 1) + 1).astype(f32)
     lane = iota((cap, clusters), 1)
 
-    @pl.loop(0, batches)
-    def _(b):
-        @pl.loop(0, batch)
-        def _(i):
+    def gather_batch(b):
+        for i in range(batch):
             step = b * batch + i
             mine = jnp.sum(
                 jnp.where(lane == owned * peer(step), held[...], 0.0), axis=1, keepdims=True
             )
-            hit = jnp.where((col + 1).astype(f32) == mine, 1.0, 0.0)
+            hit = jnp.where(col == mine, 1.0, 0.0)
             pick[pl.ds(pl.multiple_of(step * cap, cap), cap), :] = hit.astype(bf16)
 
         at = pl.ds(pl.multiple_of(b * rows_b, rows_b), rows_b)
@@ -124,38 +125,83 @@
         qk_s[at, :] = rows[:, : 2 * hd]
         v_s[at, :] = rows[:, 2 * hd :]
 
+    def send_qk(step):
+        remote(block(qk_s, step, cap), block(qk_r, me, cap), send_sem.at[1], qk_sem,
+               {"seq": peer(step)}).start()
+
+    def send_v(step):
+        remote(block(v_s, step, cap), block(v_r, me, cap), send_sem.at[2], v_sem,
+               {"seq": peer(step)}).start()
+
+    loads[2].wait()
+    loads[3].wait()
+    proj[...] = jnp.dot(tokens[...], wqkv[...], preferred_element_type=f32).astype(bf16)
+    gather_batch(0)
+
+    pl.semaphore_wait(barrier, n - 1 + heads - 1)
+
+    @pl.loop(1, nz)
+    def _(dz):
+        remote(cnt_s, tab_r.at[my_x, my_z], send_sem.at[0], cnt_sem.at[0],
+               {"seq": lax.rem(my_z + dz, nz) * nx + my_x}).start()
+
+    pltpu.make_async_copy(cnt_s, tab_r.at[my_x, my_z], cnt_sem.at[0]).start()
+
+    @pl.loop(0, batch)
+    def _(step):
+        send_qk(step)
+
+    @pl.loop(1, batches - 1)
+    def _(b):
+        gather_batch(b)
+
         @pl.loop(0, batch)
         def _(i):
-            step = b * batch + i
-
-            @pl.when(step > 0)
-            def _():
-                send_qk(step)
-
-    pltpu.make_async_copy(block(qk_s, 0, cap), block(qk_r, me, cap), qk_sem).start()
-
-    @pl.loop(1, n)
+            send_qk(b * batch + i)
+
+    gather_batch(batches - 1)
+
+    @pl.loop(own_step + 1, n)
+    def _(step):
+        send_qk(step)
+
+    pltpu.make_async_copy(block(qk_s, own_step, cap), block(qk_r, me, cap), qk_sem).start()
+
+    column = tab_r.at[my_x]
+    pltpu.make_async_copy(column, column, cnt_sem.at[0]).wait()
+
+    @pl.loop(1, nx)
+    def _(dx):
+        remote(column, column, send_sem.at[6], cnt_sem.at[1],
+               {"seq": my_z * nx + lax.rem(my_x + dx, nx)}).start()
+
+    @pl.loop(0, own_step)
     def _(step):
         send_v(step)
 
-    pltpu.make_async_copy(block(v_s, 0, cap), block(v_r, me, cap), v_sem).start()
+    @pl.loop(own_step + 1, n)
+    def _(step):
+        send_v(step)
+
+    pltpu.make_async_copy(block(v_s, own_step, cap), block(v_r, me, cap), v_sem).start()
 
     @pl.loop(1, heads)
     def _(step):
-        remote(wo, block(wo_r, my_head, hd), send_sem.at[3], wo_sem,
+        remote(wo, block(all_wo, my_head, hd), send_sem.at[3], wo_sem,
                {"head": lax.rem(my_head + step, heads)}).start()
 
-    pltpu.make_async_copy(wo, block(wo_r, my_head, hd), wo_sem).start()
+    pltpu.make_async_copy(wo, block(all_wo, my_head, hd), wo_sem).start()
 
     for b in range(batches):
         part = pick[b * rows_b : (b + 1) * rows_b, :].astype(f32)
         put[:, b * rows_b : (b + 1) * rows_b] = part.T.astype(bf16)
 
-    pltpu.make_async_copy(tab_r, tab_r, cnt_sem).wait()
+    others = tab_r.at[pl.ds(0, nx - 1)]
+    pltpu.make_async_copy(others, others, cnt_sem.at[1]).wait()
 
     @pl.loop(0, n)
     def _(s):
-        tab[pl.ds(s, 1), :] = tab_r[s]
+        tab[pl.ds(s, 1), :] = tab_r[lax.rem(s, nx), s // nx]
 
     table = tab[...].astype(bf16)
 
@@ -207,7 +253,7 @@
 
     @pl.loop(0, batches)
     def _(b):
-        turn = lax.rem(my_z * nx // batch + 3 * b, batches)
+        turn = lax.rem(my_pair + 2 * pairs - offset(b), pairs)
         at = pl.ds(pl.multiple_of(turn * rows_b, rows_b), rows_b)
         o_s[at, :] = jnp.dot(probs[at, :], v_r[...], preferred_element_type=f32).astype(bf16)
 
@@ -215,19 +261,20 @@
         def _(i):
             s = turn * batch + i
             step = (
-                lax.rem(7 * lax.rem(my_z - s // nx + nz, nz), nz) * nx
+                b * batch
+                + lax.rem(my_z + s // nx, 2) * nx
                 + lax.rem(my_x - lax.rem(s, nx) + nx, nx)
             )
 
             @pl.when(s != me)
             def _():
                 remote(block(o_s, s, cap), block(o_r, step, cap), send_sem.at[4],
-                       o_sem.at[step // batch], {"seq": s}).start()
+                       o_sem.at[b], {"seq": s}).start()
 
             @pl.when(s == me)
             def _():
                 pltpu.make_async_copy(
-                    block(o_s, s, cap), block(o_r, step, cap), o_sem.at[step // batch]
+                    block(o_s, s, cap), block(o_r, step, cap), o_sem.at[b]
                 ).start()
 
     acc[...] = jnp.zeros_like(acc)
@@ -237,28 +284,32 @@
         acc[...] += jnp.dot(put[:, b * rows_b : (b + 1) * rows_b], o_r[at, :],
                             preferred_element_type=f32)
     hs[...] = acc[...].astype(bf16)
+    lanes = all_heads.at[:, pl.ds(pl.multiple_of(my_head * hd, hd), hd)]
 
     @pl.loop(1, heads)
     def _(step):
         to = lax.rem(my_head + step, heads)
-        remote(block(hs, to, out_rows), hr.at[my_head], send_sem.at[5], h_sem,
-               {"head": to}).start()
-
-    pltpu.make_async_copy(block(hs, my_head, out_rows), hr.at[my_head], h_sem).start()
-    pltpu.make_async_copy(wo_r, wo_r, wo_sem).wait()
-    pltpu.make_async_copy(hr, hr, h_sem).wait()
-    all_heads = jnp.concatenate([hr[h] for h in range(heads)], axis=1)
-    mixed[...] = jnp.dot(all_heads, wo_r[...], preferred_element_type=f32).astype(bf16)
+        remote(block(hs, to, out_rows), lanes, send_sem.at[5], h_sem, {"head": to}).start()
+
+    pltpu.make_async_copy(block(hs, my_head, out_rows), lanes, h_sem).start()
+    pltpu.make_async_copy(all_wo, all_wo, wo_sem).wait()
+    pltpu.make_async_copy(all_heads, all_heads, h_sem).wait()
 
     def sent(ref, index):
         pltpu.make_async_copy(ref, ref, send_sem.at[index]).wait()
 
-    sent(tab_r.at[pl.ds(0, n - 1)], 0)
+    sent(tab_r.at[0, pl.ds(0, nz - 1)], 0)
+    sent(others, 6)
     sent(qk_s.at[pl.ds(0, (n - 1) * cap), :], 1)
     sent(v_s.at[pl.ds(0, (n - 1) * cap), :], 2)
-    sent(wo_r.at[pl.ds(0, (heads - 1) * hd), :], 3)
+    sent(all_wo.at[pl.ds(0, (heads - 1) * hd), :], 3)
     sent(o_s.at[pl.ds(0, (n - 1) * cap), :], 4)
-    sent(hr.at[pl.ds(0, heads - 1)], 5)
+    sent(hs.at[pl.ds(0, (heads - 1) * out_rows), :], 5)
+
+
+def mix_kernel(all_heads, all_wo, cent_in, mixed, cent):
+    mixed[...] = jnp.dot(all_heads[...], all_wo[...], preferred_element_type=f32).astype(bf16)
+    cent[...] = cent_in[...]
 
 
 def on_device(nx, tokens, qkv_weight, out_weight, members, counts):
@@ -268,17 +319,26 @@
     clusters, s_c = members.shape[1], members.shape[2]
     cap = 2 * slab // n
     rows = n * cap
-    batch = min(8, n // 2)
+    batch = 2 * nx
     vm = lambda shape, dtype: pltpu.VMEM(shape, dtype)
-    mixed, centroids = pl.pallas_call(
+    all_heads, all_wo, centroids = pl.pallas_call(
         functools.partial(layer_kernel, nx, batch, 128),
         out_shape=(
-            jax.ShapeDtypeStruct((slab // heads, width), bf16),
+            jax.ShapeDtypeStruct((slab // heads, heads * hd), bf16),
+            jax.ShapeDtypeStruct((heads * hd, width), bf16),
             jax.ShapeDtypeStruct((clusters // n, hd), f32),
         ),
-        in_specs=[pl.BlockSpec(memory_space=pltpu.VMEM)] * 5,
-        out_specs=(pl.BlockSpec(memory_space=pltpu.VMEM),) * 2,
+        in_specs=[pl.BlockSpec(memory_space=pltpu.HBM)] * 5,
+        out_specs=(
+            pl.BlockSpec(memory_space=pltpu.HBM),
+            pl.BlockSpec(memory_space=pltpu.HBM),
+            pl.BlockSpec(memory_space=pltpu.VMEM),
+        ),
         scratch_shapes=[
+            vm((slab, width), bf16),
+            vm((width, 3 * hd), bf16),
+            vm((s_c, 1, clusters), i32),
+            vm((1, clusters), i32),
             vm((slab, 3 * hd), bf16),
             vm((rows, slab), bf16),
             vm((slab, rows), bf16),
@@ -291,15 +351,14 @@
             vm((rows, hd), bf16),
             vm((slab, hd), f32),
             vm((slab, hd), bf16),
-            vm((heads, slab // heads, hd), bf16),
-            vm((heads * hd, width), bf16),
             vm((1, clusters), f32),
-            vm((n, 1, clusters), f32),
+            vm((nx, n // nx, 1, clusters), f32),
             vm((n, clusters), f32),
             vm((cap, clusters), f32),
             vm((rows, 1), f32),
-            pltpu.SemaphoreType.DMA((6,)),
-            pltpu.SemaphoreType.DMA,
+            pltpu.SemaphoreType.DMA((4,)),
+            pltpu.SemaphoreType.DMA((7,)),
+            pltpu.SemaphoreType.DMA((2,)),
             pltpu.SemaphoreType.DMA,
             pltpu.SemaphoreType.DMA,
             pltpu.SemaphoreType.DMA((n // batch,)),
@@ -313,9 +372,28 @@
         tokens,
         qkv_weight.reshape(width, 3 * hd),
         out_weight.reshape(hd, width),
-        members.reshape(clusters, s_c).T,
+        jnp.transpose(members, (2, 0, 1)),
         counts.reshape(1, clusters),
     )
+    steps = 4
+    block = width // steps
+    mixed, centroids = pl.pallas_call(
+        mix_kernel,
+        grid=(steps,),
+        out_shape=(
+            jax.ShapeDtypeStruct((slab // heads, width), bf16),
+            jax.ShapeDtypeStruct(centroids.shape, f32),
+        ),
+        in_specs=[
+            pl.BlockSpec(all_heads.shape, lambda i: (0, 0)),
+            pl.BlockSpec((heads * hd, block), lambda i: (0, i)),
+            pl.BlockSpec(centroids.shape, lambda i: (0, 0)),
+        ],
+        out_specs=(
+            pl.BlockSpec((slab // heads, block), lambda i: (0, i)),
+            pl.BlockSpec(centroids.shape, lambda i: (0, 0)),
+        ),
+    )(all_heads, all_wo, centroids)
     return mixed, centroids[None]
 
 

time: 135 us -> 127 us (0.941)
  local copies, waits for them, and re-layouts: 4.23 us -> 0 us
  Pallas kernels: 130 us -> 126 us
    pallas_call x1, Pallas kernels: 130 us -> 122 us  [on_device(): pl.pallas_call(functools.partial(layer_kernel, nx, batch, 128), out_shape...]
    unnamed x3 -> x0, local copies, waits for them, and re-layouts: 4.23 us -> none
    pallas_call x0 -> x1, Pallas kernels: none -> 3.95 us  [on_device(): pl.pallas_call(mix_kernel, grid=(steps,), out_shape=(jax.ShapeDtypeStruct...]
where the time goes in v2:
time: 127 us
  Pallas kernels  126 us (99%)
    pallas_call x1, Pallas kernels, on_device(): pl.pallas_call(functools.partial(layer_kernel, nx, batch, 128), out_shape...  122 us
    pallas_call x1, Pallas kernels, on_device(): pl.pallas_call(mix_kernel, grid=(steps,), out_shape=(jax.ShapeDtypeStruct...  3.95 us

profile of v2, /device:TPU:1, one launch (start us, length us, event | category | flops | bytes accessed | tf_op | source)
XLA Modules:
  0.0 126.9 jit_solution(9377511811169848681)
XLA Ops:
  0.6 122.3 %shard_map.68 = (bf16[128,1024]{1,0:T(8,128)(2,1)}, bf16[1024,1024]{1,0:T(8,128)(2,1)}, f32[4,128]{1,0:T(4,128)}) custom-call(bf16[1024,1024]{1,0:T(8,128)(2,1)} %tokens_hbm.1, bf16[1024,384]{1,0:T(8,128)(2,1)} %bitcast.5, bf16[128,1024]{1,0:T(8,128)(2,1)} %bitcast.6, s32[12,1,256]{2,1,0:T(1,128)} %bitcast.7, s32[1,256]{1,0:T(1,128)} %bitcast.8), custom_call_target="tpu_custom_call" | custom-call | tf_op jit(solution)/shard_map/pallas_call | solution.py:324
  123.0 4.0 %shard_map.69 = (bf16[128,1024]{1,0:T(8,128)(2,1)}, f32[4,128]{1,0:T(4,128)}) custom-call(bf16[128,1024]{1,0:T(8,128)(2,1)} %get-tuple-element.7.all_heads, bf16[1024,1024]{1,0:T(8,128)(2,1)} %get-tuple-element.8.all_wo, f32[4,128]{1,0:T(4,128)} %get-tuple-element.9.cent_in), custom_call_target="tpu_custom_call" | custom-call | tf_op jit(solution)/shard_map/pallas_call | solution.py:380

commit v3 on v2

--- a/solution.py
+++ b/solution.py
@@ -307,9 +307,20 @@
     sent(hs.at[pl.ds(0, (heads - 1) * out_rows), :], 5)
 
 
-def mix_kernel(all_heads, all_wo, cent_in, mixed, cent):
-    mixed[...] = jnp.dot(all_heads[...], all_wo[...], preferred_element_type=f32).astype(bf16)
-    cent[...] = cent_in[...]
+def mix_kernel(all_heads, all_wo, cent_in, mixed_hbm, cent_hbm, mixed, sems):
+    parts = sems.shape[0] - 1
+    size = mixed.shape[1] // parts
+    copies = [pltpu.make_async_copy(cent_in, cent_hbm, sems.at[parts])]
+    copies[0].start()
+    for c in range(parts):
+        at = pl.ds(c * size, size)
+        mixed[:, at] = jnp.dot(
+            all_heads[...], all_wo[:, at], preferred_element_type=f32
+        ).astype(bf16)
+        copies.append(pltpu.make_async_copy(mixed.at[:, at], mixed_hbm.at[:, at], sems.at[c]))
+        copies[-1].start()
+    for copy in copies:
+        copy.wait()
 
 
 def on_device(nx, tokens, qkv_weight, out_weight, members, counts):
@@ -324,14 +335,14 @@
     all_heads, all_wo, centroids = pl.pallas_call(
         functools.partial(layer_kernel, nx, batch, 128),
         out_shape=(
-            jax.ShapeDtypeStruct((slab // heads, heads * hd), bf16),
-            jax.ShapeDtypeStruct((heads * hd, width), bf16),
-            jax.ShapeDtypeStruct((clusters // n, hd), f32),
+            vm((slab // heads, heads * hd), bf16),
+            vm((heads * hd, width), bf16),
+            vm((clusters // n, hd), f32),
         ),
         in_specs=[pl.BlockSpec(memory_space=pltpu.HBM)] * 5,
         out_specs=(
-            pl.BlockSpec(memory_space=pltpu.HBM),
-            pl.BlockSpec(memory_space=pltpu.HBM),
+            pl.BlockSpec(memory_space=pltpu.VMEM),
+            pl.BlockSpec(memory_space=pltpu.VMEM),
             pl.BlockSpec(memory_space=pltpu.VMEM),
         ),
         scratch_shapes=[
@@ -366,34 +377,34 @@
             pltpu.SemaphoreType.DMA,
         ],
         compiler_params=pltpu.CompilerParams(
-            collective_id=0, has_side_effects=True, vmem_limit_bytes=56 << 20
+            collective_id=0, has_side_effects=True, vmem_limit_bytes=44 << 20
         ),
     )(
-        tokens,
-        qkv_weight.reshape(width, 3 * hd),
-        out_weight.reshape(hd, width),
-        jnp.transpose(members, (2, 0, 1)),
-        counts.reshape(1, clusters),
-    )
-    steps = 4
-    block = width // steps
+        *(
+            pltpu.with_memory_space_constraint(x, pltpu.HBM)
+            for x in (
+                tokens,
+                qkv_weight.reshape(width, 3 * hd),
+                out_weight.reshape(hd, width),
+                jnp.transpose(members, (2, 0, 1)),
+                counts.reshape(1, clusters),
+            )
+        )
+    )
+    parts = 2
     mixed, centroids = pl.pallas_call(
         mix_kernel,
-        grid=(steps,),
         out_shape=(
             jax.ShapeDtypeStruct((slab // heads, width), bf16),
             jax.ShapeDtypeStruct(centroids.shape, f32),
         ),
-        in_specs=[
-            pl.BlockSpec(all_heads.shape, lambda i: (0, 0)),
-            pl.BlockSpec((heads * hd, block), lambda i: (0, i)),
-            pl.BlockSpec(centroids.shape, lambda i: (0, 0)),
+        in_specs=[pl.BlockSpec(memory_space=pltpu.VMEM)] * 3,
+        out_specs=(pl.BlockSpec(memory_space=pltpu.HBM),) * 2,
+        scratch_shapes=[
+            vm((slab // heads, width), bf16),
+            pltpu.SemaphoreType.DMA((parts + 1,)),
         ],
-        out_specs=(
-            pl.BlockSpec((slab // heads, block), lambda i: (0, i)),
-            pl.BlockSpec(centroids.shape, lambda i: (0, 0)),
-        ),
-    )(all_heads, all_wo, centroids)
+    )(*(pltpu.with_memory_space_constraint(x, pltpu.VMEM) for x in (all_heads, all_wo, centroids)))
     return mixed, centroids[None]
 
 

time: 127 us -> 124 us (0.976)
  Pallas kernels: 126 us -> 123 us
    pallas_call x1, Pallas kernels: 3.95 us -> 1.14 us  [on_device(): pl.pallas_call(mix_kernel, out_shape=(jax.ShapeDtypeStruct((slab // heads...]
where the time goes in v3:
time: 124 us; the launch traced here: 123 us
  Pallas kernels  123 us (99%)
    pallas_call x1, Pallas kernels, on_device(): pl.pallas_call(functools.partial(layer_kernel, nx, batch, 128), out_shape...  122 us

profile of v3, /device:TPU:1, one launch (start us, length us, event | category | flops | bytes accessed | tf_op | source)
XLA Modules:
  0.0 123.4 jit_solution(5412625774774629012)
XLA Ops:
  0.6 121.6 %shard_map.68 = (bf16[128,1024]{1,0:T(8,128)(2,1)S(1)}, bf16[1024,1024]{1,0:T(8,128)(2,1)S(1)}, f32[4,128]{1,0:T(4,128)S(1)}) custom-call(bf16[1024,1024]{1,0:T(8,128)(2,1)} %tokens_hbm.1, bf16[1024,384]{1,0:T(8,128)(2,1)} %bitcast.5, bf16[128,1024]{1,0:T(8,128)(2,1)} %bitcast.6, s32[12,1,256]{2,1,0:T(1,128)} %bitcast.7, s32[1,256]{1,0:T(1,128)} %bitcast.8), custom_call_target="tpu_custom_call" | custom-call | tf_op jit(solution)/shard_map/pallas_call | solution.py:335
  122.3 1.1 shard_map.69

commit v4 on v3

--- a/solution.py
+++ b/solution.py
@@ -251,8 +251,15 @@
 
     pltpu.make_async_copy(v_r, v_r, v_sem).wait()
 
+    def batch_of(apart):
+        half = pairs // 2
+        return jnp.where(apart < half, 2 * (half - apart) - 1, 2 * (apart - half))
+
+    first = batch_of(my_pair)
+
     @pl.loop(0, batches)
-    def _(b):
+    def _(k):
+        b = jnp.where(k == 0, first, jnp.where(k <= first, k - 1, k))
         turn = lax.rem(my_pair + 2 * pairs - offset(b), pairs)
         at = pl.ds(pl.multiple_of(turn * rows_b, rows_b), rows_b)
         o_s[at, :] = jnp.dot(probs[at, :], v_r[...], preferred_element_type=f32).astype(bf16)

time: 124 us -> 121 us (0.976)
  the two profiles are of different devices: /device:TPU:1 before, /device:TPU:65 now
where the time goes in v4:
time: 121 us
  Pallas kernels  120 us (99%)
    pallas_call x1, Pallas kernels, on_device(): pl.pallas_call(functools.partial(layer_kernel, nx, batch, 128), out_shape...  119 us

profile of v4, /device:TPU:65, one launch (start us, length us, event | category | flops | bytes accessed | tf_op | source)
XLA Modules:
  0.0 120.9 jit_solution(11873194474210087673)
XLA Ops:
  0.6 119.1 %shard_map.68 = (bf16[128,1024]{1,0:T(8,128)(2,1)S(1)}, bf16[1024,1024]{1,0:T(8,128)(2,1)S(1)}, f32[4,128]{1,0:T(4,128)S(1)}) custom-call(bf16[1024,1024]{1,0:T(8,128)(2,1)} %tokens_hbm.1, bf16[1024,384]{1,0:T(8,128)(2,1)} %bitcast.5, bf16[128,1024]{1,0:T(8,128)(2,1)} %bitcast.6, s32[12,1,256]{2,1,0:T(1,128)} %bitcast.7, s32[1,256]{1,0:T(1,128)} %bitcast.8), custom_call_target="tpu_custom_call" | custom-call | tf_op jit(solution)/shard_map/pallas_call | solution.py:342
  119.7 1.1 shard_map.69

commit v5 on v4

--- a/solution.py
+++ b/solution.py
@@ -285,19 +285,30 @@
                 ).start()
 
     acc[...] = jnp.zeros_like(acc)
-    for b in range(batches):
+
+    def returned(b):
         at = pl.ds(b * rows_b, rows_b)
         pltpu.make_async_copy(o_r.at[at, :], o_r.at[at, :], o_sem.at[b]).wait()
-        acc[...] += jnp.dot(put[:, b * rows_b : (b + 1) * rows_b], o_r[at, :],
-                            preferred_element_type=f32)
-    hs[...] = acc[...].astype(bf16)
+        return at
+
+    for b in range(batches - 1):
+        at = returned(b)
+        acc[...] += jnp.dot(put[:, at], o_r[at, :], preferred_element_type=f32)
+
+    at = returned(batches - 1)
     lanes = all_heads.at[:, pl.ds(pl.multiple_of(my_head * hd, hd), hd)]
 
-    @pl.loop(1, heads)
-    def _(step):
+    def finish(to):
+        tokens_at = pl.ds(pl.multiple_of(to * out_rows, out_rows), out_rows)
+        rest = jnp.dot(put[tokens_at, at], o_r[at, :], preferred_element_type=f32)
+        hs[tokens_at, :] = (acc[tokens_at, :] + rest).astype(bf16)
+
+    for step in range(1, heads):
         to = lax.rem(my_head + step, heads)
+        finish(to)
         remote(block(hs, to, out_rows), lanes, send_sem.at[5], h_sem, {"head": to}).start()
 
+    finish(my_head)
     pltpu.make_async_copy(block(hs, my_head, out_rows), lanes, h_sem).start()
     pltpu.make_async_copy(all_wo, all_wo, wo_sem).wait()
     pltpu.make_async_copy(all_heads, all_heads, h_sem).wait()

time: 121 us -> 121 us (level)
  the two profiles are of different devices: /device:TPU:65 before, /device:TPU:97 now
where the time goes in v5:
time: 121 us
  Pallas kernels  120 us (99%)
    pallas_call x1, Pallas kernels, on_device(): pl.pallas_call(functools.partial(layer_kernel, nx, batch, 128), out_shape...  119 us

profile of v5, /device:TPU:97, one launch (start us, length us, event | category | flops | bytes accessed | tf_op | source)
XLA Modules:
  0.0 120.8 jit_solution(10119354928664382115)
XLA Ops:
  0.6 119.0 %shard_map.68 = (bf16[128,1024]{1,0:T(8,128)(2,1)S(1)}, bf16[1024,1024]{1,0:T(8,128)(2,1)S(1)}, f32[4,128]{1,0:T(4,128)S(1)}) custom-call(bf16[1024,1024]{1,0:T(8,128)(2,1)} %tokens_hbm.1, bf16[1024,384]{1,0:T(8,128)(2,1)} %bitcast.5, bf16[128,1024]{1,0:T(8,128)(2,1)} %bitcast.6, s32[12,1,256]{2,1,0:T(1,128)} %bitcast.7, s32[1,256]{1,0:T(1,128)} %bitcast.8), custom_call_target="tpu_custom_call" | custom-call | tf_op jit(solution)/shard_map/pallas_call | solution.py:353
  119.7 1.1 shard_map.69
